TPU v7x, 32 devices: a whole 2x2x4 slice. The times are simulated.
32 devices in a mesh: dom: 2 (over y), row: 4 (over z), nbr: 4 (over x, core).
Axes of the slice: x: 2, y: 2, z: 4, core: 2. Of those that a mesh axis runs over, the one named last changes fastest.
Arguments:
- blocks: float32 [24, 12, 128, 128], P(('dom', 'row'), 'nbr'), parts along dimension 0, may hold values from -0.15625 to 0.15625
- partner_ids: int32 [24, 12], P(('dom', 'row'), 'nbr'), parts along dimension 0, may hold values from 0 to 11, as said below
- counts: int32 [24], P(('dom', 'row')), parts along dimension 0, may hold values from 1 to 12, as said below
- start: float32 [3072, 32], P(('dom', 'row')), parts along dimension 0, may hold values from -6 to 6
Outputs:
- basis: float32 [3072, 32], P(('dom', 'row')), parts along dimension 0
- ritz: float32 [64, 32], P('dom'), parts along dimension 0
There are 2 independent parts, one for each index of `dom`. A program takes and returns all parts, laid end to end along the dimension named above; each array names one. Nothing has to cross between parts.
Inputs may be any that keep to these rules, and one draw needn't show every extreme that they name: partner_ids[i,0] == i; slots 1 to counts[i] - 1 hold distinct block columns greater than i; slots from counts[i] on hold i. counts[i] <= min(12, 12 - i); counts[0] == 12.
All inputs are finite; a program needn't handle non-finite values.
Results may differ from a plain program's by a relative error of at most 0.0001.
Values sent between devices are 32-bit elements; how exact they have to be, the bound alone decides.
A program may use at most 64 MiB of HBM per device.

v0:
```python
import jax
import jax.numpy as jnp
from jax import lax
from jax.sharding import PartitionSpec as P

ITERS = 2
HIGH = lax.Precision.HIGHEST


def orthonormal(image, gram, total):
    lower = jnp.linalg.cholesky(gram / total)
    return lax.linalg.triangular_solve(lower, image, left_side=False, lower=True, transpose_a=True)


def body(blocks, partner_ids, counts, start):
    block_rows, slots_here = partner_ids.shape
    block_size = blocks.shape[2]
    columns = start.shape[1]
    row_count = lax.axis_size("row")
    all_blocks = block_rows * row_count
    total = all_blocks * block_size
    first_row = lax.axis_index("row") * block_rows
    rows_here = first_row + jnp.arange(block_rows, dtype=jnp.int32)
    slot_index = lax.axis_index("nbr") * slots_here + jnp.arange(slots_here, dtype=jnp.int32)
    valid = slot_index[None, :] < counts[:, None]
    weight = jnp.where(valid, jnp.where(partner_ids == rows_here[:, None], 0.5, 1.0), 0.0).astype(
        jnp.float32
    )
    targets = jnp.concatenate([partner_ids.reshape(-1), rows_here])
    whole = lax.all_gather(start, "row", axis=0, tiled=True)
    cross = jnp.zeros((columns, columns), jnp.float32)
    prior = start
    for step in range(ITERS):
        tiles = whole.reshape(all_blocks, block_size, columns)
        far = tiles[partner_ids] * weight[:, :, None, None]
        near = lax.dynamic_slice_in_dim(tiles, first_row, block_rows, 0)
        direct = jnp.einsum("ipab,ipbk->iak", blocks, far, precision=HIGH)
        transposed = (
            jnp.einsum("ipab,iak->ipbk", blocks, near, precision=HIGH) * weight[:, :, None, None]
        )
        items = jnp.concatenate(
            [transposed.reshape(block_rows * slots_here, block_size, columns), direct], axis=0
        )
        placed = jnp.zeros((all_blocks, block_size, columns), jnp.float32).at[targets].add(items)
        summed = lax.psum_scatter(
            placed.reshape(total, columns), "row", scatter_dimension=0, tiled=True
        )
        image = lax.psum(summed, "nbr")
        gram, cross = lax.psum(
            (jnp.dot(image.T, image, precision=HIGH), jnp.dot(prior.T, image, precision=HIGH)),
            "row",
        )
        cross = cross / total
        prior = orthonormal(image, gram, total)
        if step + 1 < ITERS:
            whole = lax.all_gather(prior, "row", axis=0, tiled=True)
    return (prior, cross)


def solution(mesh):
    return jax.shard_map(
        body,
        mesh=mesh,
        in_specs=(
            P(("dom", "row"), "nbr", None, None),
            P(("dom", "row"), "nbr"),
            P(("dom", "row")),
            P(("dom", "row"), None),
        ),
        out_specs=(P(("dom", "row"), None), P("dom", None)),
        check_vma=False,
    )
```

profile of v0, /device:TPU:0, one launch (start us, length us, event | category | flops | bytes accessed | tf_op | source)
XLA Modules:
  0.0 162.5 jit_solution(3839742283190382437)
XLA Ops:
  7.2 0.0 copy-start
  7.2 0.0 copy-start.1
  7.2 0.0 reduce-scatter.3.cloned.1.call-start
  7.2 0.8 concatenate.32
  8.1 0.0 copy-done.1
  8.1 0.1 reshape.123
  8.2 15.7 %all_gather.6 = f32[1536,32]{0,1:T(8,128)S(1)} all-gather(f32[384,32]{0,1:T(8,128)} %param.10), channel_id=1, replica_groups=mesh['dom'=2,'row'=4,'nbr'=4] {'row'}, dimensions={0}, use_global_device_ids=true | all-gather | bytes 245760 | tf_op jit(solution)/shard_map/all_gather | solution.py:30
  23.9 0.6 gather_fusion
  24.4 0.0 copy-start.2
  24.4 0.6 copy-done.2
  25.1 0.1 select_select_fusion.2
  25.2 0.0 copy-done
  25.2 0.5 convolution_multiply_fusion.1
  25.6 0.8 convolution_bitcast_fusion.3
  26.4 0.1 fusion.16
  26.5 1.1 scatter_fusion
  27.6 0.7 copy_bitcast_fusion.1
  28.3 0.0 reduce-scatter.3.cloned.1.call-update
  28.3 0.0 reduce-scatter.5.cloned.1.call-start
  28.4 21.0 %reduce-scatter.3.cloned.1.call-done = f32[384,32]{0,1:T(8,128)} async-done(((f32[1536,32]{0,1:T(8,128)}), f32[384,32]{0,1:T(8,128)}) %reduce-scatter.3.cloned.1.call-update) | async-done | bytes 49168 | tf_op jit(solution)/shard_map/reduce_scatter | solution.py:45
  49.4 11.0 %psum.35 = f32[384,32]{0,1:T(8,128)S(1)} all-reduce(f32[384,32]{0,1:T(8,128)} %reduce-scatter.3.cloned.1.call-done), channel_id=1, replica_groups=mesh['dom'=2,'row'=4,'nbr'=4] {'nbr'}, use_global_device_ids=true, to_apply=%region_2.3 | all-reduce | flops 12288 | bytes 98304 | tf_op jit(solution)/shard_map/psum | solution.py:48
  60.4 0.2 fusion.20
  60.6 15.9 %psum.36 = f32[32,32]{0,1:T(8,128)S(1)} all-reduce(f32[32,32]{0,1:T(8,128)S(1)} %fusion.20), channel_id=1, replica_groups=mesh['dom'=2,'row'=4,'nbr'=4] {'row'}, use_global_device_ids=true, to_apply=%region_3.4 | all-reduce | flops 1024 | bytes 8192 | tf_op jit(solution)/shard_map/psum | solution.py:49
  76.5 0.1 copy.30
  76.6 2.9 %cholesky.44 = f32[32,32]{1,0:T(8,128)S(1)} custom-call(f32[32,32]{1,0:T(8,128)S(1)} %fusion.13), custom_call_target="Cholesky" | custom-call | tf_op jit(solution)/shard_map/jit(cholesky)/cholesky | solution.py:11
  79.5 0.6 compare_reduce_fusion.1
  80.2 0.7 fusion.8
  80.8 2.4 %custom-call.6 = f32[1,32,32]{1,2,0:T(8,128)S(1)} custom-call(f32[1,32,32]{2,1,0:T(8,128)S(1)} %fusion.8), custom_call_target="InvertDiagBlocksLowerTriangular" | custom-call | tf_op jit(solution)/shard_map/triangular_solve/custom-call.0 | solution.py:12
  83.3 0.3 convolution_bitcast_fusion.2
  83.5 13.6 %all_gather.7 = f32[1536,32]{0,1:T(8,128)S(1)} all-gather(f32[384,32]{0,1:T(8,128)S(1)} %convolution_bitcast_fusion.2), channel_id=1, replica_groups=mesh['dom'=2,'row'=4,'nbr'=4] {'row'}, dimensions={0}, use_global_device_ids=true | all-gather | bytes 245760 | tf_op jit(solution)/shard_map/all_gather | solution.py:56
  97.1 0.6 gather_fusion.1
  97.7 0.5 convolution_multiply_fusion
  98.2 0.8 convolution_bitcast_fusion.1
  99.0 1.1 scatter_fusion.1
  100.1 0.7 copy_bitcast_fusion
  100.8 0.0 reduce-scatter.5.cloned.1.call-update
  100.8 18.8 %reduce-scatter.5.cloned.1.call-done = f32[384,32]{0,1:T(8,128)} async-done(((f32[1536,32]{0,1:T(8,128)}), f32[384,32]{0,1:T(8,128)}) %reduce-scatter.5.cloned.1.call-update) | async-done | bytes 49168 | tf_op jit(solution)/shard_map/reduce_scatter | solution.py:45
  119.6 11.0 %psum.37 = f32[384,32]{0,1:T(8,128)S(1)} all-reduce(f32[384,32]{0,1:T(8,128)} %reduce-scatter.5.cloned.1.call-done), channel_id=1, replica_groups=mesh['dom'=2,'row'=4,'nbr'=4] {'nbr'}, use_global_device_ids=true, to_apply=%region_8.11 | all-reduce | flops 12288 | bytes 98304 | tf_op jit(solution)/shard_map/psum | solution.py:48
  130.6 0.2 fusion.22
  130.8 0.2 fusion.21
  131.0 16.2 %all-reduce = (f32[32,32]{0,1:T(8,128)S(1)}, f32[32,32]{0,1:T(8,128)S(1)}) all-reduce(f32[32,32]{0,1:T(8,128)S(1)} %fusion.21, f32[32,32]{0,1:T(8,128)S(1)} %fusion.22), channel_id=1, replica_groups=mesh['dom'=2,'row'=4,'nbr'=4] {'row'}, use_global_device_ids=true, to_apply=%region_9.12 | all-reduce | flops 2048 | bytes 16384 | tf_op jit(solution)/shard_map/psum | solution.py:49
  147.3 0.7 copy.37
  148.0 0.1 copy.35
  148.0 2.9 %cholesky.55 = f32[32,32]{1,0:T(8,128)S(1)} custom-call(f32[32,32]{1,0:T(8,128)S(1)} %fusion.11), custom_call_target="Cholesky" | custom-call | tf_op jit(solution)/shard_map/jit(cholesky)/cholesky | solution.py:11
  151.0 0.6 compare_reduce_fusion
  151.6 0.7 fusion.9
  152.3 2.4 %custom-call.7 = f32[1,32,32]{1,2,0:T(8,128)S(1)} custom-call(f32[1,32,32]{2,1,0:T(8,128)S(1)} %fusion.9), custom_call_target="InvertDiagBlocksLowerTriangular" | custom-call | tf_op jit(solution)/shard_map/triangular_solve/custom-call.0 | solution.py:12
  154.7 0.9 convolution_bitcast_fusion
  (17 shorter events, 0.2 us)
Async XLA Ops:
  7.2 18.0 %copy-start = (f32[3,3,128,128]{3,2,1,0:T(8,128)S(1)}, f32[3,3,128,128]{3,2,1,0:T(8,128)}, u32[]{:S(2)}) copy-start(f32[3,3,128,128]{3,2,1,0:T(8,128)} %param.7) | copy-start | bytes 1769476
  7.2 0.9 copy-start.1
  7.2 42.2 %reduce-scatter.3.cloned.1.call-start = ((), (), s32[]{:S(2)}) async-start(), calls=%async_computation.2 | async-start | bytes 245760 | tf_op jit(solution)/shard_map/reduce_scatter | solution.py:45
  24.4 0.7 copy-start.2
  28.3 91.3 %reduce-scatter.5.cloned.1.call-start = ((), (), s32[]{:S(2)}) async-start(), calls=%async_computation.3 | async-start | bytes 245760 | tf_op jit(solution)/shard_map/reduce_scatter | solution.py:45
Sparse Core Ops, SparseCore 0:
  28.4 20.9 reduce-scatter.2
  100.9 18.6 reduce-scatter.4
where the time goes:
time: 163 us; the launch traced here: 162 us
  blocking collectives  83.4 us (51%)
  waiting for transfers between devices  39.9 us (24%)
  other arithmetic  15.8 us (10%)
  between operations  14.3 us (9%)
  local copies, waits for them, and re-layouts  4.93 us (3%)
  matrix products  4.18 us (3%)
    reduce_scatter x2, waiting for transfers between devices, body(): lax.psum_scatter(placed.reshape(total, columns), 'row', scatter_dimension...  39.8 us
    psum x2, blocking collectives, body(): lax.psum((jnp.dot(image.T, image, precision=HIGH), jnp.dot(prior.T, image...  32.1 us
    psum x2, blocking collectives, body(): image = lax.psum(summed, 'nbr')  22 us
    all_gather x1, blocking collectives, body(): whole = lax.all_gather(start, 'row', axis=0, tiled=True)  15.7 us
    all_gather x1, blocking collectives, body(): whole = lax.all_gather(prior, 'row', axis=0, tiled=True)  13.6 us
    another operation x6, other arithmetic, orthonormal(): lower = jnp.linalg.cholesky(gram / total)  7.19 us
    another operation x4, other arithmetic, orthonormal(): lax.linalg.triangular_solve(lower, image, left_side=False, lower=True, tr...  6.17 us
  transfers between devices with their start and end apart: 2, of which 2 were waited for; matrix products, arithmetic and copies ran while one was open for 0% of the time, Pallas kernels for 0%

commit v1 on v0

--- a/solution.py
+++ b/solution.py
@@ -1,3 +1,4 @@
+import functools
 import jax
 import jax.numpy as jnp
 from jax import lax
@@ -5,6 +6,21 @@
 
 ITERS = 2
 HIGH = lax.Precision.HIGHEST
+
+
+def load_the_surface(s0, chip_axis):
+    degree = lax.axis_size(chip_axis)
+    entries = list(map(lambda dev: (dev, (dev + 1) % degree), range(degree)))
+    f_now = [None] * degree
+    f_now[degree - 1] = s0
+    for k0 in range(degree - 2, -1, -1):
+        f_now[k0] = lax.ppermute(f_now[k0 + 1], chip_axis, entries)
+    z_new = jnp.concatenate(f_now, axis=0)
+    y1 = jnp.roll(z_new, (lax.axis_index(chip_axis) + 1) * s0.shape[0], 0)
+    return y1
+
+
+review_tables = functools.partial(load_the_surface, chip_axis="row")
 
 
 def orthonormal(image, gram, total):
@@ -27,7 +43,7 @@
         jnp.float32
     )
     targets = jnp.concatenate([partner_ids.reshape(-1), rows_here])
-    whole = lax.all_gather(start, "row", axis=0, tiled=True)
+    whole = review_tables(start)
     cross = jnp.zeros((columns, columns), jnp.float32)
     prior = start
     for step in range(ITERS):

time: 163 us -> 163 us (level)
  blocking collectives: 83.4 us -> 67.6 us
  waiting for transfers between devices: 39.9 us -> 51.4 us
  starting transfers between devices: 0.08 us -> 3.19 us
    all_gather x1 -> x0, blocking collectives: 15.7 us -> none  [body(): whole = lax.all_gather(start, 'row', axis=0, tiled=True)]
    ppermute x0 -> x3, waiting for transfers between devices: none -> 14.4 us  [load_the_surface(): f_now[k0] = lax.ppermute(f_now[k0 + 1], chip_axis, entries)]
    ppermute x0 -> x3, starting transfers between devices: none -> 3.11 us  [load_the_surface(): f_now[k0] = lax.ppermute(f_now[k0 + 1], chip_axis, entries)]
    reduce_scatter x2, waiting for transfers between devices: 39.8 us -> 36.9 us  [body(): lax.psum_scatter(placed.reshape(total, columns), 'row', scatter_dimension...]
  transfers between devices with their start and end apart: 2 -> 5, of which waited for: 2 -> 5; matrix products, arithmetic and copies ran while one was open for 0% -> 0% of each run, Pallas kernels for 0% -> 0%
where the time goes in v1:
time: 163 us; the launch traced here: 162 us
  blocking collectives  67.6 us (41%)
  waiting for transfers between devices  51.4 us (32%)
  other arithmetic  15.8 us (10%)
  between operations  14.3 us (9%)
  local copies, waits for them, and re-layouts  5.81 us (4%)
  matrix products  4.2 us (3%)
  starting transfers between devices  3.19 us (2%)
    reduce_scatter x2, waiting for transfers between devices, body(): lax.psum_scatter(placed.reshape(total, columns), 'row', scatter_dimension...  36.9 us
    psum x2, blocking collectives, body(): lax.psum((jnp.dot(image.T, image, precision=HIGH), jnp.dot(prior.T, image...  32 us
    psum x2, blocking collectives, body(): image = lax.psum(summed, 'nbr')  22 us
    ppermute x3, waiting for transfers between devices, load_the_surface(): f_now[k0] = lax.ppermute(f_now[k0 + 1], chip_axis, entries)  14.4 us
    all_gather x1, blocking collectives, body(): whole = lax.all_gather(prior, 'row', axis=0, tiled=True)  13.6 us
    another operation x6, other arithmetic, orthonormal(): lower = jnp.linalg.cholesky(gram / total)  7.19 us
    another operation x4, other arithmetic, orthonormal(): lax.linalg.triangular_solve(lower, image, left_side=False, lower=True, tr...  6.17 us
  transfers between devices with their start and end apart: 5, of which 5 were waited for; matrix products, arithmetic and copies ran while one was open for 0% of the time, Pallas kernels for 0%

profile of v1, /device:TPU:0, one launch (start us, length us, event | category | flops | bytes accessed | tf_op | source)
XLA Modules:
  0.0 162.2 jit_solution(13400582840526321598)
XLA Ops:
  7.2 0.0 copy-start
  7.2 0.0 reduce-scatter.3.cloned.1.call-start
  7.2 3.1 %collective-permute-start = (f32[384,32]{0,1:T(8,128)}, f32[384,32]{0,1:T(8,128)S(1)}, u32[]{:S(2)}, u32[]{:S(2)}) collective-permute-start(f32[384,32]{0,1:T(8,128)} %param.10), channel_id=1, source_target_pairs={{0,4},{4,8},{8,12},{12,0},{1,5},{5,9},{9,13},{13,1},{2,6},{6,10},{... | collective-permute-start | bytes 147464 | tf_op jit(solution)/shard_map/ppermute | solution.py:17
  10.3 0.0 copy-start.2
  10.3 0.7 copy-done.2
  11.0 0.1 reshape.123
  11.1 0.0 copy-start.3
  11.1 0.7 copy-done.3
  11.8 0.1 select_select_fusion.2
  11.8 2.8 %collective-permute-done = f32[384,32]{0,1:T(8,128)S(1)} collective-permute-done((f32[384,32]{0,1:T(8,128)}, f32[384,32]{0,1:T(8,128)S(1)}, u32[]{:S(2)}, u32[]{:S(2)}) %collective-permute-start) | collective-permute-done | bytes 49184 | tf_op jit(solution)/shard_map/ppermute | solution.py:17
  14.6 0.0 collective-permute-start.1
  14.6 0.1 concatenate.38
  14.7 5.8 %collective-permute-done.1 = f32[384,32]{0,1:T(8,128)S(1)} collective-permute-done((f32[384,32]{0,1:T(8,128)S(1)}, f32[384,32]{0,1:T(8,128)S(1)}, u32[]{:S(2)}, u32[]{:S(2)}) %collective-permute-start.1) | collective-permute-done | bytes 49184 | tf_op jit(solution)/shard_map/ppermute | solution.py:17
  20.5 0.0 collective-permute-start.2
  20.5 0.1 fusion.18
  20.6 5.8 %collective-permute-done.2 = f32[384,32]{0,1:T(8,128)S(1)} collective-permute-done((f32[384,32]{0,1:T(8,128)S(1)}, f32[384,32]{0,1:T(8,128)S(1)}, u32[]{:S(2)}, u32[]{:S(2)}) %collective-permute-start.2) | collective-permute-done | bytes 49184 | tf_op jit(solution)/shard_map/ppermute | solution.py:17
  26.4 0.0 copy-start.1
  26.5 0.8 copy-done.1
  27.3 0.1 copy_bitcast_fusion.3
  27.4 0.6 gather_fusion
  28.0 0.0 copy-done
  28.0 0.5 convolution_multiply_fusion.1
  28.5 0.8 convolution_bitcast_fusion.3
  29.3 1.1 scatter_fusion
  30.4 0.7 copy_bitcast_fusion.1
  31.1 0.0 reduce-scatter.3.cloned.1.call-update
  31.1 0.0 reduce-scatter.5.cloned.1.call-start
  31.1 18.1 %reduce-scatter.3.cloned.1.call-done = f32[384,32]{0,1:T(8,128)} async-done(((f32[1536,32]{0,1:T(8,128)}), f32[384,32]{0,1:T(8,128)}) %reduce-scatter.3.cloned.1.call-update) | async-done | bytes 49168 | tf_op jit(solution)/shard_map/reduce_scatter | solution.py:61
  49.3 11.0 %psum.35 = f32[384,32]{0,1:T(8,128)S(1)} all-reduce(f32[384,32]{0,1:T(8,128)} %reduce-scatter.3.cloned.1.call-done), channel_id=1, replica_groups=mesh['dom'=2,'row'=4,'nbr'=4] {'nbr'}, use_global_device_ids=true, to_apply=%region_2.3 | all-reduce | flops 12288 | bytes 98304 | tf_op jit(solution)/shard_map/psum | solution.py:64
  60.3 0.2 fusion.20
  60.5 15.8 %psum.36 = f32[32,32]{0,1:T(8,128)S(1)} all-reduce(f32[32,32]{0,1:T(8,128)S(1)} %fusion.20), channel_id=1, replica_groups=mesh['dom'=2,'row'=4,'nbr'=4] {'row'}, use_global_device_ids=true, to_apply=%region_3.4 | all-reduce | flops 1024 | bytes 8192 | tf_op jit(solution)/shard_map/psum | solution.py:65
  76.3 0.1 copy.30
  76.4 2.9 %cholesky.44 = f32[32,32]{1,0:T(8,128)S(1)} custom-call(f32[32,32]{1,0:T(8,128)S(1)} %fusion.13), custom_call_target="Cholesky" | custom-call | tf_op jit(solution)/shard_map/jit(cholesky)/cholesky | solution.py:27
  79.4 0.6 compare_reduce_fusion.1
  80.0 0.7 fusion.8
  80.7 2.4 %custom-call.6 = f32[1,32,32]{1,2,0:T(8,128)S(1)} custom-call(f32[1,32,32]{2,1,0:T(8,128)S(1)} %fusion.8), custom_call_target="InvertDiagBlocksLowerTriangular" | custom-call | tf_op jit(solution)/shard_map/triangular_solve/custom-call.0 | solution.py:28
  83.1 0.3 convolution_bitcast_fusion.2
  83.4 13.6 %all_gather.3 = f32[1536,32]{0,1:T(8,128)S(1)} all-gather(f32[384,32]{0,1:T(8,128)S(1)} %convolution_bitcast_fusion.2), channel_id=1, replica_groups=mesh['dom'=2,'row'=4,'nbr'=4] {'row'}, dimensions={0}, use_global_device_ids=true | all-gather | bytes 245760 | tf_op jit(solution)/shard_map/all_gather | solution.py:72
  97.0 0.6 gather_fusion.1
  97.5 0.5 convolution_multiply_fusion
  98.0 0.8 convolution_bitcast_fusion.1
  98.8 1.1 scatter_fusion.1
  99.9 0.7 copy_bitcast_fusion
  100.6 0.0 reduce-scatter.5.cloned.1.call-update
  100.6 18.8 %reduce-scatter.5.cloned.1.call-done = f32[384,32]{0,1:T(8,128)} async-done(((f32[1536,32]{0,1:T(8,128)}), f32[384,32]{0,1:T(8,128)}) %reduce-scatter.5.cloned.1.call-update) | async-done | bytes 49168 | tf_op jit(solution)/shard_map/reduce_scatter | solution.py:61
  119.4 11.0 %psum.37 = f32[384,32]{0,1:T(8,128)S(1)} all-reduce(f32[384,32]{0,1:T(8,128)} %reduce-scatter.5.cloned.1.call-done), channel_id=1, replica_groups=mesh['dom'=2,'row'=4,'nbr'=4] {'nbr'}, use_global_device_ids=true, to_apply=%region_8.11 | all-reduce | flops 12288 | bytes 98304 | tf_op jit(solution)/shard_map/psum | solution.py:64
  130.5 0.2 fusion.22
  130.6 0.2 fusion.21
  130.8 16.2 %all-reduce = (f32[32,32]{0,1:T(8,128)S(1)}, f32[32,32]{0,1:T(8,128)S(1)}) all-reduce(f32[32,32]{0,1:T(8,128)S(1)} %fusion.21, f32[32,32]{0,1:T(8,128)S(1)} %fusion.22), channel_id=1, replica_groups=mesh['dom'=2,'row'=4,'nbr'=4] {'row'}, use_global_device_ids=true, to_apply=%region_9.12 | all-reduce | flops 2048 | bytes 16384 | tf_op jit(solution)/shard_map/psum | solution.py:65
  147.0 0.1 copy.35
  147.1 2.9 %cholesky.55 = f32[32,32]{1,0:T(8,128)S(1)} custom-call(f32[32,32]{1,0:T(8,128)S(1)} %fusion.11), custom_call_target="Cholesky" | custom-call | tf_op jit(solution)/shard_map/jit(cholesky)/cholesky | solution.py:27
  150.1 0.6 compare_reduce_fusion
  150.7 0.7 fusion.9
  151.4 2.4 %custom-call.7 = f32[1,32,32]{1,2,0:T(8,128)S(1)} custom-call(f32[1,32,32]{2,1,0:T(8,128)S(1)} %fusion.9), custom_call_target="InvertDiagBlocksLowerTriangular" | custom-call | tf_op jit(solution)/shard_map/triangular_solve/custom-call.0 | solution.py:28
  153.8 0.9 convolution_bitcast_fusion
  154.7 0.7 copy.37
  (24 shorter events, 0.2 us)
Async XLA Ops:
  7.2 20.8 %copy-start = (f32[3,3,128,128]{3,2,1,0:T(8,128)S(1)}, f32[3,3,128,128]{3,2,1,0:T(8,128)}, u32[]{:S(2)}) copy-start(f32[3,3,128,128]{3,2,1,0:T(8,128)} %param.7) | copy-start | bytes 1769476
  7.2 42.1 %reduce-scatter.3.cloned.1.call-start = ((), (), s32[]{:S(2)}) async-start(), calls=%async_computation.2 | async-start | bytes 245760 | tf_op jit(solution)/shard_map/reduce_scatter | solution.py:61
  7.2 7.4 %collective-permute-start = (f32[384,32]{0,1:T(8,128)}, f32[384,32]{0,1:T(8,128)S(1)}, u32[]{:S(2)}, u32[]{:S(2)}) collective-permute-start(f32[384,32]{0,1:T(8,128)} %param.10), channel_id=1, source_target_pairs={{0,4},{4,8},{8,12},{12,0},{1,5},{5,9},{9,13},{13,1},{2,6},{6,10},{... | collective-permute-start | bytes 147464 | tf_op jit(solution)/shard_map/ppermute | solution.py:17
  10.3 0.7 copy-start.2
  11.1 0.7 copy-start.3
  14.6 5.9 %collective-permute-start.1 = (f32[384,32]{0,1:T(8,128)S(1)}, f32[384,32]{0,1:T(8,128)S(1)}, u32[]{:S(2)}, u32[]{:S(2)}) collective-permute-start(f32[384,32]{0,1:T(8,128)S(1)} %collective-permute-done), channel_id=1, source_target_pairs={{0,4},{4,8},{8,12},{12,0},{1,5},{5,9},{9,13},{13,1},{2,6},{6,10},{... | collective-permute-start | bytes 147464 | tf_op jit(solution)/shard_map/ppermute | solution.py:17
  20.5 5.9 %collective-permute-start.2 = (f32[384,32]{0,1:T(8,128)S(1)}, f32[384,32]{0,1:T(8,128)S(1)}, u32[]{:S(2)}, u32[]{:S(2)}) collective-permute-start(f32[384,32]{0,1:T(8,128)S(1)} %collective-permute-done.1), channel_id=1, source_target_pairs={{0,4},{4,8},{8,12},{12,0},{1,5},{5,9},{9,13},{13,1},{2,6},{6,10},{... | collective-permute-start | bytes 147464 | tf_op jit(solution)/shard_map/ppermute | solution.py:17
  26.4 0.8 copy-start.1
  31.1 88.3 %reduce-scatter.5.cloned.1.call-start = ((), (), s32[]{:S(2)}) async-start(), calls=%async_computation.3 | async-start | bytes 245760 | tf_op jit(solution)/shard_map/reduce_scatter | solution.py:61
Sparse Core Ops, SparseCore 0:
  31.2 18.0 reduce-scatter.2
  100.7 18.6 reduce-scatter.4
